TPU v7x, 32 devices: a whole 2x2x4 slice. The times are simulated.
32 devices in a mesh: groups: 2 (over y), blk: 4 (over z), oct: 2 (over x), sub: 2 (over core).
Axes of the slice: x: 2, y: 2, z: 4, core: 2. Of those that a mesh axis runs over, the one named last changes fastest.
Arguments:
- positions: float32 [3, 65536], P(None, ('groups', 'blk', 'oct', 'sub')), parts along dimension 1, may hold values from 0 to 320
- polarizability: float32 [65536], P(('groups', 'blk', 'oct', 'sub')), parts along dimension 0, may hold values from 0.5 to 1.5
- permanent_field: float32 [3, 65536], P(None, ('groups', 'blk', 'oct', 'sub')), parts along dimension 1, may hold values from -40 to 40
- group_id: int32 [65536], P(('groups', 'blk', 'oct', 'sub')), parts along dimension 0, may hold values from 0 to 10921, never falling along the last dimension, each value on 1 to 6 neighbouring positions
- pair_mask: int32 [512, 9], P(('groups', 'blk', 'oct', 'sub')), parts along dimension 0, may hold values from 0 to 1, as said below
Outputs:
- dipoles: float32 [3, 65536], P(None, ('groups', 'blk', 'oct', 'sub')), parts along dimension 1
- residual: float32 [3, 65536], P(None, ('groups', 'blk', 'oct', 'sub')), parts along dimension 1
There are 2 independent parts, one for each index of `groups`. A program takes and returns all parts, laid end to end along the dimension named above; each array names one. Nothing has to cross between parts.
Inputs may be any that keep to these rules, and one draw needn't show every extreme that they name: `group_id`: never falls from one atom to the next; each value names 1 to 6 consecutive atoms. pair_mask[b, 4] = 1, and pair_mask[b, 4 + o] = pair_mask[(b + o) mod 256, 4 - o].
All inputs are finite; a program needn't handle non-finite values.
Results may differ from a plain program's by a relative error of at most 0.0003.
Values sent between devices are 32-bit elements; how exact they have to be, the bound alone decides.
No kernel may reach another device: no remote copies, remote signals or barrier semaphores. Data moves between devices by JAX's collectives and lax.ppermute only.
A program may use at most 64 MiB of HBM per device.

v0:
```python
import math
import jax
import jax.numpy as jnp
import numpy as np
from jax import lax
from jax.sharding import PartitionSpec as P

BOXES_DEV = 2
BLOCK = 128
ORDER = 5
NODE_PAD = 128
ITERS = 2
side_length = 32.0
layer_gap = 2.5
thole_damp = 0.39
highest = lax.Precision.HIGHEST


def padded(cells, sides, width):
    for axis, dim in sides:
        count = lax.axis_size(axis)
        head = lax.slice_in_dim(cells, 0, width, axis=dim)
        tail = lax.slice_in_dim(cells, cells.shape[dim] - width, cells.shape[dim], axis=dim)
        cells = jnp.concatenate(
            [
                lax.ppermute(tail, axis, [(i, (i + 1) % count) for i in range(count)]),
                cells,
                lax.ppermute(head, axis, [((i + 1) % count, i) for i in range(count)]),
            ],
            axis=dim,
        )
    return cells


def wrap_image(delta, period):
    return delta - period * jnp.floor(delta / period + 0.5)


def split_size(total, limit):
    best = 1
    for factor in range(1, min(total, limit) + 1):
        if total % factor == 0:
            best = factor
    return best


def near_tiles(target, source, moments, keep_tile, length_z):
    delta_x = wrap_image(target[0][:, :, None] - source[0][:, None, :], side_length)
    delta_y = wrap_image(target[1][:, :, None] - source[1][:, None, :], side_length)
    delta_z = wrap_image(target[2][:, :, None] - source[2][:, None, :], length_z)
    keep = (keep_tile[:, None, None] > 0.5) & (target[4][:, :, None] != source[4][:, None, :])
    dist_sq = jnp.where(keep, delta_x * delta_x + delta_y * delta_y + delta_z * delta_z, 1.0)
    inv_three = lax.rsqrt(dist_sq) / dist_sq
    scaled = (
        thole_damp
        * dist_sq
        * jnp.sqrt(dist_sq)
        * lax.rsqrt(target[3][:, :, None] * source[3][:, None, :])
    )
    lam_three = -jnp.expm1(-scaled)
    lam_five = lam_three - scaled * jnp.exp(-scaled)
    coef_five = jnp.where(keep, 3.0 * lam_five * inv_three / dist_sq, 0.0)
    coef_three = jnp.where(keep, lam_three * inv_three, 0.0)
    along = (
        delta_x * moments[0][:, None, :]
        + delta_y * moments[1][:, None, :]
        + delta_z * moments[2][:, None, :]
    )
    weighted = coef_five * along
    field_x = jnp.sum(weighted * delta_x - coef_three * moments[0][:, None, :], axis=2)
    field_y = jnp.sum(weighted * delta_y - coef_three * moments[1][:, None, :], axis=2)
    field_z = jnp.sum(weighted * delta_z - coef_three * moments[2][:, None, :], axis=2)
    return jnp.stack([field_x, field_y, field_z])


def near_total(static_ext, dipole_ext, mask_rows, length_z, atom_count):
    reach = (mask_rows.shape[1] - 1) // 2
    width = reach * BLOCK
    blocks = atom_count // BLOCK
    target = static_ext[:, width : width + atom_count].reshape(5, blocks, BLOCK)
    total = jnp.zeros((3, blocks, BLOCK), static_ext.dtype)
    for offset in range(-reach, reach + 1):
        begin = (reach + offset) * BLOCK
        source = static_ext[:, begin : begin + atom_count].reshape(5, blocks, BLOCK)
        moments = dipole_ext[:, begin : begin + atom_count].reshape(3, blocks, BLOCK)
        keep_tile = mask_rows[:, reach + offset].astype(static_ext.dtype)
        total = total + near_tiles(target, source, moments, keep_tile, length_z)
    return total.reshape(3, atom_count)


def node_tables():
    count = ORDER
    roots = np.cos((2.0 * np.arange(count) + 1.0) * np.pi / (2.0 * count))
    degree = np.arange(count)
    coeff = (
        2.0 / count * np.cos(np.outer(2.0 * np.arange(count) + 1.0, degree) * np.pi / (2.0 * count))
    )
    coeff = np.where(degree[None, :] == 0, 1.0 / count, coeff)
    index = np.arange(NODE_PAD)
    live = index < count**3
    safe = np.where(live, index, 0)
    first = safe // (count * count)
    second = safe // count % count
    third = safe % count
    levels = np.arange(count)[None, :]
    pick_a = (first[:, None] == levels) * live[:, None] * 1.0
    pick_b = (second[:, None] == levels) * 1.0
    pick_c = (third[:, None] == levels) * 1.0
    node_x = 16.0 * (1.0 + roots[first])
    node_y = 16.0 * (1.0 + roots[second])
    node_t = roots[third]
    tables = [coeff, pick_a, pick_b, pick_c, node_x, node_y, node_t]
    return [jnp.asarray(item, jnp.float32) for item in tables]


def interpolation(coords, box_ids, box_height):
    coeff, pick_a, pick_b, pick_c, node_x, node_y, node_t = node_tables()
    scaled_x = coords[0] / 16.0 - 1.0
    scaled_y = coords[1] / 16.0 - 1.0
    scaled_z = (
        2.0 * (coords[2] - box_ids.astype(coords.dtype)[:, None] * box_height) / box_height - 1.0
    )

    def basis(values, picks):
        terms = [jnp.ones_like(values), values]
        for degree in range(2, ORDER):
            terms.append(2.0 * values * terms[-1] - terms[-2])
        stacked = jnp.stack(terms[:ORDER])
        smooth = jnp.einsum("kn,nba->kba", coeff, stacked, precision=highest)
        return jnp.einsum("pk,kba->pba", picks, smooth, precision=highest)

    return basis(scaled_x, pick_a) * basis(scaled_y, pick_b) * basis(scaled_z, pick_c)


def far_block(target_ids, source_ids, weights, slabs, box_height, length_z):
    coeff, pick_a, pick_b, pick_c, node_x, node_y, node_t = node_tables()
    height_t = (
        target_ids.astype(weights.dtype)[:, None] * box_height
        + 0.5 * box_height * (1.0 + node_t)[None, :]
    )
    height_s = (
        source_ids.astype(weights.dtype)[:, None] * box_height
        + 0.5 * box_height * (1.0 + node_t)[None, :]
    )
    delta_x = wrap_image(node_x[:, None] - node_x[None, :], side_length)[None, :, None, :]
    delta_y = wrap_image(node_y[:, None] - node_y[None, :], side_length)[None, :, None, :]
    delta_z = wrap_image(height_t[:, :, None, None] - height_s[None, None, :, :], length_z)
    apart = jnp.abs(target_ids[:, None] // BOXES_DEV - source_ids[None, :] // BOXES_DEV)
    apart = jnp.minimum(apart, slabs - apart)
    keep = (apart >= 1)[:, None, :, None]
    dist_sq = jnp.where(
        keep,
        delta_x * delta_x + delta_y * delta_y + delta_z * delta_z + box_height * box_height,
        1.0,
    )
    inv_three = lax.rsqrt(dist_sq) / dist_sq
    coef_five = jnp.where(keep, 3.0 * inv_three / dist_sq, 0.0)
    coef_three = jnp.where(keep, inv_three, 0.0)
    weight_x = weights[:, 0, :][None, None]
    weight_y = weights[:, 1, :][None, None]
    weight_z = weights[:, 2, :][None, None]
    weighted = coef_five * (delta_x * weight_x + delta_y * weight_y + delta_z * weight_z)
    field_x = jnp.sum(weighted * delta_x - coef_three * weight_x, axis=(2, 3))
    field_y = jnp.sum(weighted * delta_y - coef_three * weight_y, axis=(2, 3))
    field_z = jnp.sum(weighted * delta_z - coef_three * weight_z, axis=(2, 3))
    return jnp.stack([field_x, field_y, field_z], axis=1)


def on_device(positions, polarizability, permanent_field, group_id, pair_mask):
    slabs = lax.axis_size(("blk", "oct", "sub"))
    member = lax.axis_index(("blk", "oct", "sub"))
    atom_count = positions.shape[1]
    length_z = layer_gap * atom_count * slabs / 256.0
    box_height = length_z / (BOXES_DEV * slabs)
    per_box = atom_count // BOXES_DEV
    width = (pair_mask.shape[1] - 1) // 2 * BLOCK
    group_limit = max(1, 32 // BOXES_DEV)
    static = jnp.concatenate(
        [positions, polarizability[None, :], group_id.astype(jnp.float32)[None, :]], axis=0
    )
    static_ext = padded(static, ((("blk", "oct", "sub"), 1),), width)
    own_boxes = member * BOXES_DEV + jnp.arange(BOXES_DEV, dtype=jnp.int32)
    interp = interpolation(positions.reshape(3, BOXES_DEV, per_box), own_boxes, box_height)
    surface = 4.0 * math.pi / 3.0 / (side_length * side_length * length_z)

    def induced(dipoles, total):
        dipole_ext = padded(dipoles, ((("blk", "oct", "sub"), 1),), width)
        near = near_total(static_ext, dipole_ext, pair_mask, length_z, atom_count)
        weights = jnp.einsum(
            "pba,cba->bcp", interp, dipoles.reshape(3, BOXES_DEV, per_box), precision=highest
        )
        piece = lax.all_gather(weights, ("blk", "oct", "sub"), axis=0, tiled=True)
        start = jnp.int32(0)
        count = piece.shape[0]
        size = split_size(count, group_limit)
        grouped = piece.reshape(count // size, size, 3, piece.shape[2])

        def visit(acc, item):
            index, bundle = item
            sources = start + index * size + jnp.arange(size, dtype=jnp.int32)
            return (acc + far_block(own_boxes, sources, bundle, slabs, box_height, length_z), None)

        result, unused = lax.scan(
            visit, jnp.zeros_like(weights), (jnp.arange(count // size, dtype=jnp.int32), grouped)
        )
        far = jnp.einsum("pba,bcp->cba", interp, result, precision=highest).reshape(3, atom_count)
        return near + far - surface * total[:, None]

    def moment(values):
        return lax.psum(jnp.sum(values, axis=1), ("blk", "oct", "sub"))

    def squares(resid, scaled):
        return lax.psum(jnp.sum(resid * scaled), ("blk", "oct", "sub"))

    dipoles = polarizability[None, :] * permanent_field
    residual = induced(dipoles, moment(dipoles))
    precond = polarizability[None, :] * residual
    direction = precond
    norm_now = squares(residual, precond)
    for step in range(ITERS):
        image = direction / polarizability[None, :] - induced(direction, moment(direction))
        rate = norm_now / lax.psum(jnp.sum(direction * image), ("blk", "oct", "sub"))
        dipoles = dipoles + rate * direction
        residual = residual - rate * image
        if step + 1 < ITERS:
            precond = polarizability[None, :] * residual
            norm_next = squares(residual, precond)
            direction = precond + norm_next / norm_now * direction
            norm_now = norm_next
    return (dipoles, residual)


def solution(mesh):
    return jax.shard_map(
        on_device,
        mesh=mesh,
        in_specs=(
            P(None, ("groups", "blk", "oct", "sub")),
            P(("groups", "blk", "oct", "sub")),
            P(None, ("groups", "blk", "oct", "sub")),
            P(("groups", "blk", "oct", "sub")),
            P(("groups", "blk", "oct", "sub"), None),
        ),
        out_specs=(
            P(None, ("groups", "blk", "oct", "sub")),
            P(None, ("groups", "blk", "oct", "sub")),
        ),
        check_vma=False,
    )
```

profile of v0, /device:TPU:0, one launch (start us, length us, event | category | flops | bytes accessed | tf_op | source)
XLA Modules:
  0.0 428.3 jit_solution(15247812564218952183)
XLA Ops:
  2.6 5.0 %collective-permute-start.2 = (f32[5,512]{1,0:T(8,128)S(1)}, f32[5,512]{1,0:T(8,128)S(1)}, u32[]{:S(2)}, u32[]{:S(2)}) collective-permute-start(f32[5,512]{1,0:T(8,128)S(1)} %get-tuple-element.990), channel_id=1, source_target_pairs={{1,0},{2,1},{3,2},{4,3},{5,4},{6,5},{7,6},{8,7},{9,8},{10,9},{11,1... | collective-permute-start | bytes 30728 | tf_op jit(solution)/shard_map/ppermute | solution.py:28
  14.0 29.5 %psum.49 = f32[3]{0:T(128)S(1)} all-reduce(f32[3]{0:T(128)S(1)} %get-tuple-element.927), channel_id=1, replica_groups=mesh['groups'=2,'blk'=4,'oct'=2,'sub'=2] {'blk','oct','sub'}, use_global_device_ids=true, to_apply=%region_33.34 | all-reduce | flops 3 | bytes 24 | tf_op jit(solution)/shard_map/psum | solution.py:210
  52.0 17.8 %all_gather.9 = f32[32,3,128]{2,1,0:T(4,128)S(1)} all-gather(f32[2,3,128]{2,1,0:T(4,128)S(1)} %fusion.782), channel_id=1, replica_groups=mesh['groups'=2,'blk'=4,'oct'=2,'sub'=2] {'blk','oct','sub'}, dimensions={0}, use_global_device_ids=true | all-gather | bytes 52224 | tf_op jit(solution)/shard_map/all_gather | solution.py:192
  69.9 13.5 %while.51 = (s32[]{:T(128)}, f32[2,3,128]{2,0,1:T(2,128)S(1)}, s32[2]{0:T(128)S(1)}, f32[2,16,3,128]{3,1,2,0:T(8,128)S(1)}, s32[]{:T(128)}, /*index=5*/s32[]{:T(...) while((s32[]{:T(128)}, f32[2,3,128]{2,0,1:T(2,128)S(1)}, ...), condition=%wide.region_31.32_spmd.clone.clone.clone.clone, body=%wide.region_27.31_spmd.sunk.clone.clone.clone.clone.sunk | while | flops 16765948 | bytes 2795035 | solution.py:203
  71.8 4.8 %subtract_reduce_fusion.9 = (f32[2,128]{1,0:T(2,128)S(1)}, f32[2,128]{1,0:T(2,128)S(1)}, f32[2,128]{1,0:T(2,128)S(1)}) fusion(f32[16,128]{1,0:T(8,128)S(1)} %get-tuple-element.1216, f32[128,128]{1,0:T(8,128)S(1)} %get-tuple-element.1217, pred[2,16]{1,0:T(4,128)(4,1)S(1)} %fusion.814, f32[16,128]{1,0:T(8,128)S(1)} %broadcast_add_fusion.12, ...), kind=kLoop, calls=%fused_computation.28.clone.1 | loop fusion | flops 15727872 | bytes 1282080 | tf_op jit(solution)/shard_map/while/body/eval_jaxpr/reduce_sum | solution.py:163
  78.5 4.8 %subtract_reduce_fusion.9 = (f32[2,128]{1,0:T(2,128)S(1)}, f32[2,128]{1,0:T(2,128)S(1)}, f32[2,128]{1,0:T(2,128)S(1)}) fusion(f32[16,128]{1,0:T(8,128)S(1)} %get-tuple-element.1216, f32[128,128]{1,0:T(8,128)S(1)} %get-tuple-element.1217, pred[2,16]{1,0:T(4,128)(4,1)S(1)} %fusion.814, f32[16,128]{1,0:T(8,128)S(1)} %broadcast_add_fusion.12, ...), kind=kLoop, calls=%fused_computation.28.clone.1 | loop fusion | flops 15727872 | bytes 1282080 | tf_op jit(solution)/shard_map/while/body/eval_jaxpr/reduce_sum | solution.py:163
  112.2 7.3 %fusion.630 = (f32[16,128]{1,0:T(8,128)S(1)}, f32[16,128]{1,0:T(8,128)S(1)}, f32[16,128]{1,0:T(8,128)S(1)}, f32[16,128]{1,0:T(8,128)S(1)}, f32[16,128]{1,0:T(8,128)S(1)}, /*index=5*/f32[16,128]{1,0:T(8,128)S(1)}) fusion(f32[16,128]{1,0:T(8,128)S(1)} %bitcast.840, f32[16,128]{1,0:T(8,128)S(1)} %bitcast.735, f32[16,128]{1,0:T(8,128)S(1)} %bitcast.931, ...), kind=kLoop, calls=%fused_computation.815 | loop fusion | flops 30920704 | bytes 180256 | tf_op jit(solution)/shard_map/reduce_sum | solution.py:70
  120.7 31.6 %psum.51 = f32[3]{0:T(128)S(1)} all-reduce(f32[3]{0:T(128)S(1)} %get-tuple-element.923), channel_id=1, replica_groups=mesh['groups'=2,'blk'=4,'oct'=2,'sub'=2] {'blk','oct','sub'}, use_global_device_ids=true, to_apply=%region_69.70 | all-reduce | flops 3 | bytes 24 | tf_op jit(solution)/shard_map/psum | solution.py:210
  153.2 4.4 %collective-permute-start.5 = (f32[3,512]{1,0:T(4,128)S(1)}, f32[3,512]{1,0:T(4,128)S(1)}, u32[]{:S(2)}, u32[]{:S(2)}) collective-permute-start(f32[3,512]{1,0:T(4,128)S(1)} %get-tuple-element.1078), channel_id=1, source_target_pairs={{1,0},{2,1},{3,2},{4,3},{5,4},{6,5},{7,6},{8,7},{9,8},{10,9},{11,1... | collective-permute-start | bytes 18440 | tf_op jit(solution)/shard_map/ppermute | solution.py:28
  157.6 17.3 %all_gather.10 = f32[32,3,128]{2,1,0:T(4,128)S(1)} all-gather(f32[2,3,128]{2,1,0:T(4,128)S(1)} %fusion.684), channel_id=1, replica_groups=mesh['groups'=2,'blk'=4,'oct'=2,'sub'=2] {'blk','oct','sub'}, dimensions={0}, use_global_device_ids=true | all-gather | bytes 52224 | tf_op jit(solution)/shard_map/all_gather | solution.py:192
  174.9 13.0 %while.52 = (s32[]{:T(128)}, f32[2,3,128]{2,0,1:T(2,128)S(1)}, s32[2]{0:T(128)S(1)}, f32[2,16,3,128]{3,1,2,0:T(8,128)S(1)}, s32[]{:T(128)}, /*index=5*/s32[]{:T(...) while((s32[]{:T(128)}, f32[2,3,128]{2,0,1:T(2,128)S(1)}, ...), condition=%wide.region_67.68_spmd.clone.clone.clone.clone, body=%wide.region_63.67_spmd.sunk.clone.clone.clone.clone.sunk | while | flops 16765948 | bytes 2795035 | solution.py:203
  176.6 4.8 %subtract_reduce_fusion.10 = (f32[2,128]{1,0:T(2,128)S(1)}, f32[2,128]{1,0:T(2,128)S(1)}, f32[2,128]{1,0:T(2,128)S(1)}) fusion(f32[16,128]{1,0:T(8,128)S(1)} %get-tuple-element.1230, f32[128,128]{1,0:T(8,128)S(1)} %get-tuple-element.1231, pred[2,16]{1,0:T(4,128)(4,1)S(1)} %fusion.817, f32[16,128]{1,0:T(8,128)S(1)} %broadcast_add_fusion.14, ...), kind=kLoop, calls=%fused_computation.82.clone.1 | loop fusion | flops 15727872 | bytes 1282080 | tf_op jit(solution)/shard_map/while/body/eval_jaxpr/reduce_sum | solution.py:163
  183.1 4.8 %subtract_reduce_fusion.10 = (f32[2,128]{1,0:T(2,128)S(1)}, f32[2,128]{1,0:T(2,128)S(1)}, f32[2,128]{1,0:T(2,128)S(1)}) fusion(f32[16,128]{1,0:T(8,128)S(1)} %get-tuple-element.1230, f32[128,128]{1,0:T(8,128)S(1)} %get-tuple-element.1231, pred[2,16]{1,0:T(4,128)(4,1)S(1)} %fusion.817, f32[16,128]{1,0:T(8,128)S(1)} %broadcast_add_fusion.14, ...), kind=kLoop, calls=%fused_computation.82.clone.1 | loop fusion | flops 15727872 | bytes 1282080 | tf_op jit(solution)/shard_map/while/body/eval_jaxpr/reduce_sum | solution.py:163
  216.1 7.3 %fusion.629 = (f32[16,128]{1,0:T(8,128)S(1)}, f32[16,128]{1,0:T(8,128)S(1)}, f32[16,128]{1,0:T(8,128)S(1)}, f32[16,128]{1,0:T(8,128)S(1)}, f32[16,128]{1,0:T(8,128)S(1)}, /*index=5*/f32[16,128]{1,0:T(8,128)S(1)}) fusion(f32[16,128]{1,0:T(8,128)S(1)} %bitcast.872, f32[16,128]{1,0:T(8,128)S(1)} %bitcast.736, f32[16,128]{1,0:T(8,128)S(1)} %bitcast.939, ...), kind=kLoop, calls=%fused_computation.814 | loop fusion | flops 30920704 | bytes 180256 | tf_op jit(solution)/shard_map/reduce_sum | solution.py:70
  225.1 32.1 %all-reduce = (f32[]{:T(128)}, f32[]{:T(128)}) all-reduce(f32[]{:T(128)} %get-tuple-element.870, f32[]{:T(128)} %get-tuple-element.869), channel_id=1, replica_groups=mesh['groups'=2,'blk'=4,'oct'=2,'sub'=2] {'blk','oct','sub'}, use_global_device_ids=true, to_apply=%region_35.36 | all-reduce | flops 2 | bytes 16 | tf_op jit(solution)/shard_map/psum | solution.py:213
  259.1 30.1 %psum.53 = f32[]{:T(128)} all-reduce(f32[]{:T(128)} %fusion.632), channel_id=1, replica_groups=mesh['groups'=2,'blk'=4,'oct'=2,'sub'=2] {'blk','oct','sub'}, use_global_device_ids=true, to_apply=%region_73.74 | all-reduce | flops 1 | bytes 8 | tf_op jit(solution)/shard_map/psum | solution.py:213
  290.6 29.7 %psum.54 = f32[3]{0:T(128)S(1)} all-reduce(f32[3]{0:T(128)S(1)} %get-tuple-element.918), channel_id=1, replica_groups=mesh['groups'=2,'blk'=4,'oct'=2,'sub'=2] {'blk','oct','sub'}, use_global_device_ids=true, to_apply=%region_107.108 | all-reduce | flops 3 | bytes 24 | tf_op jit(solution)/shard_map/psum | solution.py:210
  321.3 4.4 %collective-permute-start.7 = (f32[3,512]{1,0:T(4,128)S(1)}, f32[3,512]{1,0:T(4,128)S(1)}, u32[]{:S(2)}, u32[]{:S(2)}) collective-permute-start(f32[3,512]{1,0:T(4,128)S(1)} %get-tuple-element.1070), channel_id=1, source_target_pairs={{1,0},{2,1},{3,2},{4,3},{5,4},{6,5},{7,6},{8,7},{9,8},{10,9},{11,1... | collective-permute-start | bytes 18440 | tf_op jit(solution)/shard_map/ppermute | solution.py:28
  325.7 17.3 %all_gather.11 = f32[32,3,128]{2,1,0:T(4,128)S(1)} all-gather(f32[2,3,128]{2,1,0:T(4,128)S(1)} %fusion.783), channel_id=1, replica_groups=mesh['groups'=2,'blk'=4,'oct'=2,'sub'=2] {'blk','oct','sub'}, dimensions={0}, use_global_device_ids=true | all-gather | bytes 52224 | tf_op jit(solution)/shard_map/all_gather | solution.py:192
  343.0 13.0 %while.53 = (s32[]{:T(128)}, f32[2,3,128]{2,0,1:T(2,128)S(1)}, s32[2]{0:T(128)S(1)}, f32[2,16,3,128]{3,1,2,0:T(8,128)S(1)}, s32[]{:T(128)}, /*index=5*/s32[]{:T(...) while((s32[]{:T(128)}, f32[2,3,128]{2,0,1:T(2,128)S(1)}, ...), condition=%wide.region_105.106_spmd.clone.clone.clone.clone, body=%wide.region_101.105_spmd.sunk.clone.clone.clone.clone.sunk | while | flops 16765948 | bytes 2795035 | solution.py:203
  344.7 4.8 %subtract_reduce_fusion.11 = (f32[2,128]{1,0:T(2,128)S(1)}, f32[2,128]{1,0:T(2,128)S(1)}, f32[2,128]{1,0:T(2,128)S(1)}) fusion(f32[16,128]{1,0:T(8,128)S(1)} %get-tuple-element.1244, f32[128,128]{1,0:T(8,128)S(1)} %get-tuple-element.1245, pred[2,16]{1,0:T(4,128)(4,1)S(1)} %fusion.820, f32[16,128]{1,0:T(8,128)S(1)} %broadcast_add_fusion.16, ...), kind=kLoop, calls=%fused_computation.136.clone.1 | loop fusion | flops 15727872 | bytes 1282080 | tf_op jit(solution)/shard_map/while/body/eval_jaxpr/reduce_sum | solution.py:163
  351.2 4.8 %subtract_reduce_fusion.11 = (f32[2,128]{1,0:T(2,128)S(1)}, f32[2,128]{1,0:T(2,128)S(1)}, f32[2,128]{1,0:T(2,128)S(1)}) fusion(f32[16,128]{1,0:T(8,128)S(1)} %get-tuple-element.1244, f32[128,128]{1,0:T(8,128)S(1)} %get-tuple-element.1245, pred[2,16]{1,0:T(4,128)(4,1)S(1)} %fusion.820, f32[16,128]{1,0:T(8,128)S(1)} %broadcast_add_fusion.16, ...), kind=kLoop, calls=%fused_computation.136.clone.1 | loop fusion | flops 15727872 | bytes 1282080 | tf_op jit(solution)/shard_map/while/body/eval_jaxpr/reduce_sum | solution.py:163
  384.3 7.3 %fusion.628 = (f32[16,128]{1,0:T(8,128)S(1)}, f32[16,128]{1,0:T(8,128)S(1)}, f32[16,128]{1,0:T(8,128)S(1)}, f32[16,128]{1,0:T(8,128)S(1)}, f32[16,128]{1,0:T(8,128)S(1)}, /*index=5*/f32[16,128]{1,0:T(8,128)S(1)}) fusion(f32[16,128]{1,0:T(8,128)S(1)} %bitcast.862, f32[16,128]{1,0:T(8,128)S(1)} %bitcast.737, f32[16,128]{1,0:T(8,128)S(1)} %bitcast.947, ...), kind=kLoop, calls=%fused_computation.813 | loop fusion | flops 30920704 | bytes 180256 | tf_op jit(solution)/shard_map/reduce_sum | solution.py:70
  393.2 32.0 %psum.55 = f32[]{:T(128)} all-reduce(f32[]{:T(128)} %get-tuple-element.1104), channel_id=1, replica_groups=mesh['groups'=2,'blk'=4,'oct'=2,'sub'=2] {'blk','oct','sub'}, use_global_device_ids=true, to_apply=%region_109.110 | all-reduce | flops 1 | bytes 8 | tf_op jit(solution)/shard_map/psum | solution.py:222
  (198 shorter events, 116.9 us)
Async XLA Ops:
  0.6 45.0 %copy-start.8 = (f32[5,5,1]{1,0,2:T(8,128)S(1)}, f32[5,5,1]{1,0,2:T(8,128)}, u32[]{:S(2)}) copy-start(f32[5,5,1]{1,0,2:T(8,128)} %constant.532) | copy-start | bytes 304
  0.6 45.2 %copy-start.11 = (f32[128,5,1]{0,1,2:T(8,128)S(1)}, f32[128,5,1]{0,1,2:T(8,128)}, u32[]{:S(2)}) copy-start(f32[128,5,1]{0,1,2:T(8,128)} %constant.533) | copy-start | bytes 7684
  2.1 81.8 %collective-permute-start = (f32[5,512]{1,0:T(8,128)S(1)}, f32[5,512]{1,0:T(8,128)S(1)}, u32[]{:S(2)}, u32[]{:S(2)}) collective-permute-start(f32[5,512]{1,0:T(8,128)S(1)} %get-tuple-element.989), channel_id=1, source_target_pairs={{0,1},{1,2},{2,3},{3,4},{4,5},{5,6},{6,7},{7,8},{8,9},{9,10},{10,1... | collective-permute-start | bytes 30728 | tf_op jit(solution)/shard_map/ppermute | solution.py:26
  2.6 81.3 %collective-permute-start.2 = (f32[5,512]{1,0:T(8,128)S(1)}, f32[5,512]{1,0:T(8,128)S(1)}, u32[]{:S(2)}, u32[]{:S(2)}) collective-permute-start(f32[5,512]{1,0:T(8,128)S(1)} %get-tuple-element.990), channel_id=1, source_target_pairs={{1,0},{2,1},{3,2},{4,3},{5,4},{6,5},{7,6},{8,7},{9,8},{10,9},{11,1... | collective-permute-start | bytes 30728 | tf_op jit(solution)/shard_map/ppermute | solution.py:28
  8.6 75.2 %collective-permute-start.1 = (f32[3,512]{1,0:T(4,128)S(1)}, f32[3,512]{1,0:T(4,128)S(1)}, u32[]{:S(2)}, u32[]{:S(2)}) collective-permute-start(f32[3,512]{1,0:T(4,128)S(1)} %get-tuple-element.1085), channel_id=1, source_target_pairs={{0,1},{1,2},{2,3},{3,4},{4,5},{5,6},{6,7},{7,8},{8,9},{9,10},{10,1... | collective-permute-start | bytes 18440 | tf_op jit(solution)/shard_map/ppermute | solution.py:26
  8.6 75.2 %collective-permute-start.3 = (f32[3,512]{1,0:T(4,128)S(1)}, f32[3,512]{1,0:T(4,128)S(1)}, u32[]{:S(2)}, u32[]{:S(2)}) collective-permute-start(f32[3,512]{1,0:T(4,128)S(1)} %get-tuple-element.1086), channel_id=1, source_target_pairs={{1,0},{2,1},{3,2},{4,3},{5,4},{6,5},{7,6},{8,7},{9,8},{10,9},{11,1... | collective-permute-start | bytes 18440 | tf_op jit(solution)/shard_map/ppermute | solution.py:28
  13.1 34.7 %copy-start.10 = (f32[128,5,1]{0,1,2:T(8,128)S(1)}, f32[128,5,1]{0,1,2:T(8,128)}, u32[]{:S(2)}) copy-start(f32[128,5,1]{0,1,2:T(8,128)} %constant.534) | copy-start | bytes 7684
  47.7 1.8 copy-start.9
  51.4 18.4 %copy-start.2 = (f32[128]{0:T(128)S(1)}, f32[128]{0:T(128)}, u32[]{:S(2)}) copy-start(f32[128]{0:T(128)} %constant.2011) | copy-start | bytes 1540
  51.4 18.4 %copy-start.4 = (f32[128]{0:T(128)S(1)}, f32[128]{0:T(128)}, u32[]{:S(2)}) copy-start(f32[128]{0:T(128)} %constant.489.clone..sunk.15) | copy-start | bytes 1540
  51.4 18.4 %copy-start.5 = (f32[128]{0:T(128)S(1)}, f32[128]{0:T(128)}, u32[]{:S(2)}) copy-start(f32[128]{0:T(128)} %constant.2010) | copy-start | bytes 1540
  51.4 18.4 %copy-start.6 = (f32[128]{0:T(128)S(1)}, f32[128]{0:T(128)}, u32[]{:S(2)}) copy-start(f32[128]{0:T(128)} %constant.490.clone..sunk.15) | copy-start | bytes 1540
  51.4 18.4 %copy-start.7 = (f32[128]{0:T(128)S(1)}, f32[128]{0:T(128)}, u32[]{:S(2)}) copy-start(f32[128]{0:T(128)} %constant.2009) | copy-start | bytes 1540
  69.9 13.5 %copy-start = (s32[16,9]{1,0:T(8,128)S(1)}, s32[16,9]{1,0:T(8,128)}, u32[]{:S(2)}) copy-start(s32[16,9]{1,0:T(8,128)} %param.28) | copy-start | bytes 1732
  69.9 13.8 %copy-start.1 = (f32[2048]{0:T(1024)S(1)}, f32[2048]{0:T(1024)}, u32[]{:S(2)}) copy-start(f32[2048]{0:T(1024)} %param.25) | copy-start | bytes 24580
  69.9 14.0 %copy-start.3 = (f32[3,2048]{1,0:T(4,128)S(1)}, f32[3,2048]{1,0:T(4,128)}, u32[]{:S(2)}) copy-start(f32[3,2048]{1,0:T(4,128)} %param.24) | copy-start | bytes 73732
  153.1 34.8 %collective-permute-start.4 = (f32[3,512]{1,0:T(4,128)S(1)}, f32[3,512]{1,0:T(4,128)S(1)}, u32[]{:S(2)}, u32[]{:S(2)}) collective-permute-start(f32[3,512]{1,0:T(4,128)S(1)} %get-tuple-element.1077), channel_id=1, source_target_pairs={{0,1},{1,2},{2,3},{3,4},{4,5},{5,6},{6,7},{7,8},{8,9},{9,10},{10,1... | collective-permute-start | bytes 18440 | tf_op jit(solution)/shard_map/ppermute | solution.py:26
  153.2 34.8 %collective-permute-start.5 = (f32[3,512]{1,0:T(4,128)S(1)}, f32[3,512]{1,0:T(4,128)S(1)}, u32[]{:S(2)}, u32[]{:S(2)}) collective-permute-start(f32[3,512]{1,0:T(4,128)S(1)} %get-tuple-element.1078), channel_id=1, source_target_pairs={{1,0},{2,1},{3,2},{4,3},{5,4},{6,5},{7,6},{8,7},{9,8},{10,9},{11,1... | collective-permute-start | bytes 18440 | tf_op jit(solution)/shard_map/ppermute | solution.py:28
  321.2 34.8 %collective-permute-start.6 = (f32[3,512]{1,0:T(4,128)S(1)}, f32[3,512]{1,0:T(4,128)S(1)}, u32[]{:S(2)}, u32[]{:S(2)}) collective-permute-start(f32[3,512]{1,0:T(4,128)S(1)} %get-tuple-element.1069), channel_id=1, source_target_pairs={{0,1},{1,2},{2,3},{3,4},{4,5},{5,6},{6,7},{7,8},{8,9},{9,10},{10,1... | collective-permute-start | bytes 18440 | tf_op jit(solution)/shard_map/ppermute | solution.py:26
  321.3 34.8 %collective-permute-start.7 = (f32[3,512]{1,0:T(4,128)S(1)}, f32[3,512]{1,0:T(4,128)S(1)}, u32[]{:S(2)}, u32[]{:S(2)}) collective-permute-start(f32[3,512]{1,0:T(4,128)S(1)} %get-tuple-element.1070), channel_id=1, source_target_pairs={{1,0},{2,1},{3,2},{4,3},{5,4},{6,5},{7,6},{8,7},{9,8},{10,9},{11,1... | collective-permute-start | bytes 18440 | tf_op jit(solution)/shard_map/ppermute | solution.py:28
where the time goes:
time: 434 us; the launch traced here: 428 us
  blocking collectives  237 us (55%)
  other arithmetic  145 us (33%)
  starting transfers between devices  19 us (4%)
  matrix products  13.6 us (3%)
  between operations  5.61 us (1%)
    reduce_sum x24, other arithmetic, near_tiles(): jnp.sum(weighted * delta_x - coef_three * moments[0][:, None, :], axis=2)  106 us
    psum x3, blocking collectives, moment(): return lax.psum(jnp.sum(values, axis=1), ('blk', 'oct', 'sub'))  90.8 us
    psum x2, blocking collectives, squares(): return lax.psum(jnp.sum(resid * scaled), ('blk', 'oct', 'sub'))  62.2 us
    all_gather x3, blocking collectives, induced(): piece = lax.all_gather(weights, ('blk', 'oct', 'sub'), axis=0, tiled=True)  52.3 us
    psum x1, blocking collectives, on_device(): lax.psum(jnp.sum(direction * image), ('blk', 'oct', 'sub'))  32 us
    reduce_sum x6, other arithmetic, far_block(): field_x = jnp.sum(weighted * delta_x - coef_three * weight_x, axis=(2, 3))  28.8 us
    ppermute x4, starting transfers between devices, padded(): lax.ppermute(head, axis, [((i + 1) % count, i) for i in range(count)])  18.3 us
  transfers between devices with their start and end apart: 8, of which 0 were waited for; matrix products, arithmetic and copies ran while one was open for 11% of the time, Pallas kernels for 0%

commit v1 on v0

--- a/solution.py
+++ b/solution.py
@@ -14,6 +14,28 @@
 layer_gap = 2.5
 thole_damp = 0.39
 highest = lax.Precision.HIGHEST
+
+
+def joined_along(pieces, dim):
+    pieces = jnp.moveaxis(pieces, 0, dim)
+    dims = pieces.shape
+    return pieces.reshape(*dims[:dim], dims[dim] * dims[dim + 1], *dims[dim + 2 :])
+
+
+def grow_blocks(x, axis):
+    size = lax.axis_size(axis)
+    parts = x[None]
+    for level in range(size.bit_length() - 1):
+        stride = 1 << level
+        received = lax.ppermute(parts, axis, [(i, i ^ stride) for i in range(size)])
+        both = jnp.stack([parts, received])
+        upper = lax.axis_index(axis) >> level & 1
+        parts = jnp.where(upper == 0, both, both[::-1]).reshape(-1, *x.shape)
+    return parts
+
+
+def doubled_up(x, axis, dim):
+    return joined_along(grow_blocks(x, axis), dim)
 
 
 def padded(cells, sides, width):
@@ -189,7 +211,7 @@
         weights = jnp.einsum(
             "pba,cba->bcp", interp, dipoles.reshape(3, BOXES_DEV, per_box), precision=highest
         )
-        piece = lax.all_gather(weights, ("blk", "oct", "sub"), axis=0, tiled=True)
+        piece = doubled_up(weights, ("blk", "oct", "sub"), 0)
         start = jnp.int32(0)
         count = piece.shape[0]
         size = split_size(count, group_limit)

time: 434 us -> 395 us (0.910)
  blocking collectives: 237 us -> 188 us
  waiting for transfers between devices: 0.02 us -> 8.03 us
    all_gather x3 -> x0, blocking collectives: 52.3 us -> none  [induced(): piece = lax.all_gather(weights, ('blk', 'oct', 'sub'), axis=0, tiled=True)]
    ppermute x0 -> x12, waiting for transfers between devices: none -> 5.48 us  [grow_blocks(): received = lax.ppermute(parts, axis, [(i, i ^ stride) for i in range(size)])]
  transfers between devices with their start and end apart: 8 -> 20, of which waited for: 0 -> 8; matrix products, arithmetic and copies ran while one was open for 11% -> 30% of each run, Pallas kernels for 0% -> 0%
where the time goes in v1:
time: 395 us; the launch traced here: 389 us
  blocking collectives  188 us (48%)
  other arithmetic  145 us (37%)
  starting transfers between devices  20.2 us (5%)
  matrix products  13.6 us (3%)
  waiting for transfers between devices  8.03 us (2%)
  between operations  5.92 us (1%)
  local copies, waits for them, and re-layouts  4.23 us (1%)
  loops' own time  4.04 us (1%)
    reduce_sum x24, other arithmetic, near_tiles(): jnp.sum(weighted * delta_x - coef_three * moments[0][:, None, :], axis=2)  106 us
    psum x3, blocking collectives, moment(): return lax.psum(jnp.sum(values, axis=1), ('blk', 'oct', 'sub'))  90.1 us
    psum x2, blocking collectives, squares(): return lax.psum(jnp.sum(resid * scaled), ('blk', 'oct', 'sub'))  63.9 us
    psum x1, blocking collectives, on_device(): lax.psum(jnp.sum(direction * image), ('blk', 'oct', 'sub'))  33.8 us
    reduce_sum x6, other arithmetic, far_block(): field_x = jnp.sum(weighted * delta_x - coef_three * weight_x, axis=(2, 3))  28.8 us
    ppermute x4, starting transfers between devices, padded(): lax.ppermute(head, axis, [((i + 1) % count, i) for i in range(count)])  17.7 us
  transfers between devices with their start and end apart: 20, of which 8 were waited for; matrix products, arithmetic and copies ran while one was open for 30% of the time, Pallas kernels for 0%

profile of v1, /device:TPU:0, one launch (start us, length us, event | category | flops | bytes accessed | tf_op | source)
XLA Modules:
  0.0 388.7 jit_solution(8315216135176778362)
XLA Ops:
  2.6 5.0 %collective-permute-start.2 = (f32[5,512]{1,0:T(8,128)S(1)}, f32[5,512]{1,0:T(8,128)S(1)}, u32[]{:S(2)}, u32[]{:S(2)}) collective-permute-start(f32[5,512]{1,0:T(8,128)S(1)} %get-tuple-element.975), channel_id=1, source_target_pairs={{1,0},{2,1},{3,2},{4,3},{5,4},{6,5},{7,6},{8,7},{9,8},{10,9},{11,1... | collective-permute-start | bytes 30728 | tf_op jit(solution)/shard_map/ppermute | solution.py:50
  8.6 4.4 %collective-permute-start.3 = (f32[3,512]{1,0:T(4,128)S(1)}, f32[3,512]{1,0:T(4,128)S(1)}, u32[]{:S(2)}, u32[]{:S(2)}) collective-permute-start(f32[3,512]{1,0:T(4,128)S(1)} %get-tuple-element.1071), channel_id=1, source_target_pairs={{1,0},{2,1},{3,2},{4,3},{5,4},{6,5},{7,6},{8,7},{9,8},{10,9},{11,1... | collective-permute-start | bytes 18440 | tf_op jit(solution)/shard_map/ppermute | solution.py:50
  22.6 30.4 %psum.49 = f32[3]{0:T(128)S(1)} all-reduce(f32[3]{0:T(128)S(1)} %get-tuple-element.912), channel_id=1, replica_groups=mesh['groups'=2,'blk'=4,'oct'=2,'sub'=2] {'blk','oct','sub'}, use_global_device_ids=true, to_apply=%region_33.34 | all-reduce | flops 3 | bytes 24 | tf_op jit(solution)/shard_map/psum | solution.py:232
  77.6 7.3 %fusion.630 = (f32[16,128]{1,0:T(8,128)S(1)}, f32[16,128]{1,0:T(8,128)S(1)}, f32[16,128]{1,0:T(8,128)S(1)}, f32[16,128]{1,0:T(8,128)S(1)}, f32[16,128]{1,0:T(8,128)S(1)}, /*index=5*/f32[16,128]{1,0:T(8,128)S(1)}) fusion(f32[16,128]{1,0:T(8,128)S(1)} %bitcast.918, f32[16,128]{1,0:T(8,128)S(1)} %bitcast.849, f32[16,128]{1,0:T(8,128)S(1)} %bitcast.1004, ...), kind=kLoop, calls=%fused_computation.815 | loop fusion | flops 30920704 | bytes 180256 | tf_op jit(solution)/shard_map/reduce_sum | solution.py:92
  93.8 13.3 %while.51 = (s32[]{:T(128)}, f32[2,3,128]{2,0,1:T(2,128)S(1)}, s32[2]{0:T(128)S(1)}, f32[2,16,3,128]{3,1,2,0:T(8,128)S(1)}, s32[]{:T(128)}, /*index=5*/s32[]{:T(...) while((s32[]{:T(128)}, f32[2,3,128]{2,0,1:T(2,128)S(1)}, ...), condition=%wide.region_31.32_spmd.clone.clone.clone.clone, body=%wide.region_27.31_spmd.sunk.clone.clone.clone.clone.sunk | while | flops 16765948 | bytes 2795035 | solution.py:225
  95.6 4.8 %subtract_reduce_fusion.9 = (f32[2,128]{1,0:T(2,128)S(1)}, f32[2,128]{1,0:T(2,128)S(1)}, f32[2,128]{1,0:T(2,128)S(1)}) fusion(f32[16,128]{1,0:T(8,128)S(1)} %get-tuple-element.1207, f32[128,128]{1,0:T(8,128)S(1)} %get-tuple-element.1208, pred[2,16]{1,0:T(4,128)(4,1)S(1)} %fusion.820, f32[16,128]{1,0:T(8,128)S(1)} %broadcast_add_fusion.12, ...), kind=kLoop, calls=%fused_computation.28.clone.1 | loop fusion | flops 15727872 | bytes 1282080 | tf_op jit(solution)/shard_map/while/body/eval_jaxpr/reduce_sum | solution.py:185
  102.3 4.8 %subtract_reduce_fusion.9 = (f32[2,128]{1,0:T(2,128)S(1)}, f32[2,128]{1,0:T(2,128)S(1)}, f32[2,128]{1,0:T(2,128)S(1)}) fusion(f32[16,128]{1,0:T(8,128)S(1)} %get-tuple-element.1207, f32[128,128]{1,0:T(8,128)S(1)} %get-tuple-element.1208, pred[2,16]{1,0:T(4,128)(4,1)S(1)} %fusion.820, f32[16,128]{1,0:T(8,128)S(1)} %broadcast_add_fusion.12, ...), kind=kLoop, calls=%fused_computation.28.clone.1 | loop fusion | flops 15727872 | bytes 1282080 | tf_op jit(solution)/shard_map/while/body/eval_jaxpr/reduce_sum | solution.py:185
  108.2 30.2 %psum.51 = f32[3]{0:T(128)S(1)} all-reduce(f32[3]{0:T(128)S(1)} %get-tuple-element.908), channel_id=1, replica_groups=mesh['groups'=2,'blk'=4,'oct'=2,'sub'=2] {'blk','oct','sub'}, use_global_device_ids=true, to_apply=%region_69.70 | all-reduce | flops 3 | bytes 24 | tf_op jit(solution)/shard_map/psum | solution.py:232
  139.9 4.1 %collective-permute-start.9 = (f32[3,512]{1,0:T(4,128)S(1)}, f32[3,512]{1,0:T(4,128)S(1)}, u32[]{:S(2)}, u32[]{:S(2)}) collective-permute-start(f32[3,512]{1,0:T(4,128)S(1)} %get-tuple-element.1063), channel_id=1, source_target_pairs={{1,0},{2,1},{3,2},{4,3},{5,4},{6,5},{7,6},{8,7},{9,8},{10,9},{11,1... | collective-permute-start | bytes 18440 | tf_op jit(solution)/shard_map/ppermute | solution.py:50
  145.4 4.0 %fusion.602 = (f32[16,128]{1,0:T(8,128)S(1)}, f32[16,128]{1,0:T(8,128)S(1)}, f32[16,128]{1,0:T(8,128)S(1)}) fusion(f32[16,128]{1,0:T(8,128)S(1)} %bitcast.964, f32[16,128]{1,0:T(8,128)S(1)} %bitcast.907, f32[16,128]{1,0:T(8,128)S(1)} %bitcast.1007, f32[16,128]{1,0:T(8,128)S(1)} %bitcast.965, f32[16,128]{1,0:T(8,128)S(1)} %bitcast.963, ...), kind=kLoop, calls=%fused_computation.787 | loop fusion | flops 15460352 | bytes 131088 | tf_op jit(solution)/shard_map/reduce_sum | solution.py:92
  161.6 7.3 %fusion.629 = (f32[16,128]{1,0:T(8,128)S(1)}, f32[16,128]{1,0:T(8,128)S(1)}, f32[16,128]{1,0:T(8,128)S(1)}, f32[16,128]{1,0:T(8,128)S(1)}, f32[16,128]{1,0:T(8,128)S(1)}, /*index=5*/f32[16,128]{1,0:T(8,128)S(1)}) fusion(f32[16,128]{1,0:T(8,128)S(1)} %bitcast.956, f32[16,128]{1,0:T(8,128)S(1)} %bitcast.850, f32[16,128]{1,0:T(8,128)S(1)} %bitcast.1011, ...), kind=kLoop, calls=%fused_computation.814 | loop fusion | flops 30920704 | bytes 180256 | tf_op jit(solution)/shard_map/reduce_sum | solution.py:92
  181.9 13.2 %while.52 = (s32[]{:T(128)}, f32[2,3,128]{2,0,1:T(2,128)S(1)}, s32[2]{0:T(128)S(1)}, f32[2,16,3,128]{3,1,2,0:T(8,128)S(1)}, s32[]{:T(128)}, /*index=5*/s32[]{:T(...) while((s32[]{:T(128)}, f32[2,3,128]{2,0,1:T(2,128)S(1)}, ...), condition=%wide.region_67.68_spmd.clone.clone.clone.clone, body=%wide.region_63.67_spmd.sunk.clone.clone.clone.clone.sunk | while | flops 16765948 | bytes 2795035 | solution.py:225
  183.7 4.8 %subtract_reduce_fusion.10 = (f32[2,128]{1,0:T(2,128)S(1)}, f32[2,128]{1,0:T(2,128)S(1)}, f32[2,128]{1,0:T(2,128)S(1)}) fusion(f32[16,128]{1,0:T(8,128)S(1)} %get-tuple-element.1221, f32[128,128]{1,0:T(8,128)S(1)} %get-tuple-element.1222, pred[2,16]{1,0:T(4,128)(4,1)S(1)} %fusion.823, f32[16,128]{1,0:T(8,128)S(1)} %broadcast_add_fusion.14, ...), kind=kLoop, calls=%fused_computation.82.clone.1 | loop fusion | flops 15727872 | bytes 1282080 | tf_op jit(solution)/shard_map/while/body/eval_jaxpr/reduce_sum | solution.py:185
  190.3 4.8 %subtract_reduce_fusion.10 = (f32[2,128]{1,0:T(2,128)S(1)}, f32[2,128]{1,0:T(2,128)S(1)}, f32[2,128]{1,0:T(2,128)S(1)}) fusion(f32[16,128]{1,0:T(8,128)S(1)} %get-tuple-element.1221, f32[128,128]{1,0:T(8,128)S(1)} %get-tuple-element.1222, pred[2,16]{1,0:T(4,128)(4,1)S(1)} %fusion.823, f32[16,128]{1,0:T(8,128)S(1)} %broadcast_add_fusion.14, ...), kind=kLoop, calls=%fused_computation.82.clone.1 | loop fusion | flops 15727872 | bytes 1282080 | tf_op jit(solution)/shard_map/while/body/eval_jaxpr/reduce_sum | solution.py:185
  196.8 33.8 %all-reduce = (f32[]{:T(128)}, f32[]{:T(128)}) all-reduce(f32[]{:T(128)} %get-tuple-element.855, f32[]{:T(128)} %get-tuple-element.854), channel_id=1, replica_groups=mesh['groups'=2,'blk'=4,'oct'=2,'sub'=2] {'blk','oct','sub'}, use_global_device_ids=true, to_apply=%region_35.36 | all-reduce | flops 2 | bytes 16 | tf_op jit(solution)/shard_map/psum | solution.py:235
  232.6 30.1 %psum.53 = f32[]{:T(128)} all-reduce(f32[]{:T(128)} %fusion.632), channel_id=1, replica_groups=mesh['groups'=2,'blk'=4,'oct'=2,'sub'=2] {'blk','oct','sub'}, use_global_device_ids=true, to_apply=%region_73.74 | all-reduce | flops 1 | bytes 8 | tf_op jit(solution)/shard_map/psum | solution.py:235
  264.1 29.5 %psum.54 = f32[3]{0:T(128)S(1)} all-reduce(f32[3]{0:T(128)S(1)} %get-tuple-element.903), channel_id=1, replica_groups=mesh['groups'=2,'blk'=4,'oct'=2,'sub'=2] {'blk','oct','sub'}, use_global_device_ids=true, to_apply=%region_107.108 | all-reduce | flops 3 | bytes 24 | tf_op jit(solution)/shard_map/psum | solution.py:232
  295.1 4.2 %collective-permute-start.15 = (f32[3,512]{1,0:T(4,128)S(1)}, f32[3,512]{1,0:T(4,128)S(1)}, u32[]{:S(2)}, u32[]{:S(2)}) collective-permute-start(f32[3,512]{1,0:T(4,128)S(1)} %get-tuple-element.1055), channel_id=1, source_target_pairs={{1,0},{2,1},{3,2},{4,3},{5,4},{6,5},{7,6},{8,7},{9,8},{10,9},{11,1... | collective-permute-start | bytes 18440 | tf_op jit(solution)/shard_map/ppermute | solution.py:50
  304.7 4.0 %fusion.601 = (f32[16,128]{1,0:T(8,128)S(1)}, f32[16,128]{1,0:T(8,128)S(1)}, f32[16,128]{1,0:T(8,128)S(1)}) fusion(f32[16,128]{1,0:T(8,128)S(1)} %bitcast.950, f32[16,128]{1,0:T(8,128)S(1)} %bitcast.908, f32[16,128]{1,0:T(8,128)S(1)} %bitcast.1016, f32[16,128]{1,0:T(8,128)S(1)} %bitcast.951, f32[16,128]{1,0:T(8,128)S(1)} %bitcast.949, ...), kind=kLoop, calls=%fused_computation.786 | loop fusion | flops 15460352 | bytes 131088 | tf_op jit(solution)/shard_map/reduce_sum | solution.py:92
  316.8 7.3 %fusion.628 = (f32[16,128]{1,0:T(8,128)S(1)}, f32[16,128]{1,0:T(8,128)S(1)}, f32[16,128]{1,0:T(8,128)S(1)}, f32[16,128]{1,0:T(8,128)S(1)}, f32[16,128]{1,0:T(8,128)S(1)}, /*index=5*/f32[16,128]{1,0:T(8,128)S(1)}) fusion(f32[16,128]{1,0:T(8,128)S(1)} %bitcast.952, f32[16,128]{1,0:T(8,128)S(1)} %bitcast.851, f32[16,128]{1,0:T(8,128)S(1)} %bitcast.1019, ...), kind=kLoop, calls=%fused_computation.813 | loop fusion | flops 30920704 | bytes 180256 | tf_op jit(solution)/shard_map/reduce_sum | solution.py:92
  337.2 13.0 %while.53 = (s32[]{:T(128)}, f32[2,3,128]{2,0,1:T(2,128)S(1)}, s32[2]{0:T(128)S(1)}, f32[2,16,3,128]{3,1,2,0:T(8,128)S(1)}, s32[]{:T(128)}, /*index=5*/s32[]{:T(...) while((s32[]{:T(128)}, f32[2,3,128]{2,0,1:T(2,128)S(1)}, ...), condition=%wide.region_105.106_spmd.clone.clone.clone.clone, body=%wide.region_101.105_spmd.sunk.clone.clone.clone.clone.sunk | while | flops 16765948 | bytes 2795035 | solution.py:225
  338.9 4.8 %subtract_reduce_fusion.11 = (f32[2,128]{1,0:T(2,128)S(1)}, f32[2,128]{1,0:T(2,128)S(1)}, f32[2,128]{1,0:T(2,128)S(1)}) fusion(f32[16,128]{1,0:T(8,128)S(1)} %get-tuple-element.1235, f32[128,128]{1,0:T(8,128)S(1)} %get-tuple-element.1236, pred[2,16]{1,0:T(4,128)(4,1)S(1)} %fusion.826, f32[16,128]{1,0:T(8,128)S(1)} %broadcast_add_fusion.16, ...), kind=kLoop, calls=%fused_computation.136.clone.1 | loop fusion | flops 15727872 | bytes 1282080 | tf_op jit(solution)/shard_map/while/body/eval_jaxpr/reduce_sum | solution.py:185
  345.4 4.8 %subtract_reduce_fusion.11 = (f32[2,128]{1,0:T(2,128)S(1)}, f32[2,128]{1,0:T(2,128)S(1)}, f32[2,128]{1,0:T(2,128)S(1)}) fusion(f32[16,128]{1,0:T(8,128)S(1)} %get-tuple-element.1235, f32[128,128]{1,0:T(8,128)S(1)} %get-tuple-element.1236, pred[2,16]{1,0:T(4,128)(4,1)S(1)} %fusion.826, f32[16,128]{1,0:T(8,128)S(1)} %broadcast_add_fusion.16, ...), kind=kLoop, calls=%fused_computation.136.clone.1 | loop fusion | flops 15727872 | bytes 1282080 | tf_op jit(solution)/shard_map/while/body/eval_jaxpr/reduce_sum | solution.py:185
  351.9 33.8 %psum.55 = f32[]{:T(128)} all-reduce(f32[]{:T(128)} %get-tuple-element.1095), channel_id=1, replica_groups=mesh['groups'=2,'blk'=4,'oct'=2,'sub'=2] {'blk','oct','sub'}, use_global_device_ids=true, to_apply=%region_109.110 | all-reduce | flops 1 | bytes 8 | tf_op jit(solution)/shard_map/psum | solution.py:244
  (246 shorter events, 114.5 us)
Async XLA Ops:
  0.6 15.8 %copy-start.11 = (f32[128,5,1]{0,1,2:T(8,128)S(1)}, f32[128,5,1]{0,1,2:T(8,128)}, u32[]{:S(2)}) copy-start(f32[128,5,1]{0,1,2:T(8,128)} %constant.537) | copy-start | bytes 7684
  2.1 55.1 %collective-permute-start = (f32[5,512]{1,0:T(8,128)S(1)}, f32[5,512]{1,0:T(8,128)S(1)}, u32[]{:S(2)}, u32[]{:S(2)}) collective-permute-start(f32[5,512]{1,0:T(8,128)S(1)} %get-tuple-element.974), channel_id=1, source_target_pairs={{0,1},{1,2},{2,3},{3,4},{4,5},{5,6},{6,7},{7,8},{8,9},{9,10},{10,1... | collective-permute-start | bytes 30728 | tf_op jit(solution)/shard_map/ppermute | solution.py:48
  2.6 54.6 %collective-permute-start.2 = (f32[5,512]{1,0:T(8,128)S(1)}, f32[5,512]{1,0:T(8,128)S(1)}, u32[]{:S(2)}, u32[]{:S(2)}) collective-permute-start(f32[5,512]{1,0:T(8,128)S(1)} %get-tuple-element.975), channel_id=1, source_target_pairs={{1,0},{2,1},{3,2},{4,3},{5,4},{6,5},{7,6},{8,7},{9,8},{10,9},{11,1... | collective-permute-start | bytes 30728 | tf_op jit(solution)/shard_map/ppermute | solution.py:50
  8.6 44.9 %collective-permute-start.1 = (f32[3,512]{1,0:T(4,128)S(1)}, f32[3,512]{1,0:T(4,128)S(1)}, u32[]{:S(2)}, u32[]{:S(2)}) collective-permute-start(f32[3,512]{1,0:T(4,128)S(1)} %get-tuple-element.1070), channel_id=1, source_target_pairs={{0,1},{1,2},{2,3},{3,4},{4,5},{5,6},{6,7},{7,8},{8,9},{9,10},{10,1... | collective-permute-start | bytes 18440 | tf_op jit(solution)/shard_map/ppermute | solution.py:48
  8.6 44.9 %collective-permute-start.3 = (f32[3,512]{1,0:T(4,128)S(1)}, f32[3,512]{1,0:T(4,128)S(1)}, u32[]{:S(2)}, u32[]{:S(2)}) collective-permute-start(f32[3,512]{1,0:T(4,128)S(1)} %get-tuple-element.1071), channel_id=1, source_target_pairs={{1,0},{2,1},{3,2},{4,3},{5,4},{6,5},{7,6},{8,7},{9,8},{10,9},{11,1... | collective-permute-start | bytes 18440 | tf_op jit(solution)/shard_map/ppermute | solution.py:50
  21.9 31.1 %copy-start = (s32[16,9]{1,0:T(8,128)S(1)}, s32[16,9]{1,0:T(8,128)}, u32[]{:S(2)}) copy-start(s32[16,9]{1,0:T(8,128)} %param.28) | copy-start | bytes 1732
  21.9 31.5 %copy-start.1 = (f32[2048]{0:T(1024)S(1)}, f32[2048]{0:T(1024)}, u32[]{:S(2)}) copy-start(f32[2048]{0:T(1024)} %param.25) | copy-start | bytes 24580
  21.9 35.3 %copy-start.3 = (f32[3,2048]{1,0:T(4,128)S(1)}, f32[3,2048]{1,0:T(4,128)}, u32[]{:S(2)}) copy-start(f32[3,2048]{1,0:T(4,128)} %param.24) | copy-start | bytes 73732
  22.5 30.9 %collective-permute-start.4 = (f32[1,2,3,128]{3,2,1,0:T(4,128)S(1)}, f32[1,2,3,128]{3,2,1,0:T(4,128)S(1)}, u32[]{:S(2)}, u32[]{:S(2)}) collective-permute-start(f32[1,2,3,128]{3,2,1,0:T(4,128)S(1)} %bitcast.766), channel_id=1, source_target_pairs={{0,1},{1,0},{2,3},{3,2},{4,5},{5,4},{6,7},{7,6},{8,9},{9,8},{10,11... | collective-permute-start | bytes 9224 | tf_op jit(solution)/shard_map/ppermute | solution.py:30
  53.4 3.7 collective-permute-start.5
  57.2 31.7 %collective-permute-start.6 = (f32[4,2,3,128]{3,2,1,0:T(4,128)S(1)}, f32[4,2,3,128]{3,2,1,0:T(4,128)S(1)}, u32[]{:S(2)}, u32[]{:S(2)}) collective-permute-start(f32[4,2,3,128]{3,2,1,0:T(4,128)S(1)} %bitcast.566), channel_id=1, source_target_pairs={{0,4},{1,5},{2,6},{3,7},{4,0},{5,1},{6,2},{7,3},{8,12},{9,13},{10,... | collective-permute-start | bytes 36872 | tf_op jit(solution)/shard_map/ppermute | solution.py:30
  88.9 4.8 %collective-permute-start.7 = (f32[8,2,3,128]{3,1,0,2:T(2,128)S(1)}, f32[8,2,3,128]{3,1,0,2:T(2,128)S(1)}, u32[]{:S(2)}, u32[]{:S(2)}) collective-permute-start(f32[8,2,3,128]{3,1,0,2:T(2,128)S(1)} %copy.39), channel_id=1, source_target_pairs={{0,8},{1,9},{2,10},{3,11},{4,12},{5,13},{6,14},{7,15},{8,0},{9,1},... | collective-permute-start | bytes 73736 | tf_op jit(solution)/shard_map/ppermute | solution.py:30
  139.0 5.0 %collective-permute-start.10 = (f32[1,2,3,128]{3,2,1,0:T(4,128)S(1)}, f32[1,2,3,128]{3,2,1,0:T(4,128)S(1)}, u32[]{:S(2)}, u32[]{:S(2)}) collective-permute-start(f32[1,2,3,128]{3,2,1,0:T(4,128)S(1)} %bitcast.764), channel_id=1, source_target_pairs={{0,1},{1,0},{2,3},{3,2},{4,5},{5,4},{6,7},{7,6},{8,9},{9,8},{10,11... | collective-permute-start | bytes 9224 | tf_op jit(solution)/shard_map/ppermute | solution.py:30
  139.4 5.8 %collective-permute-start.8 = (f32[3,512]{1,0:T(4,128)S(1)}, f32[3,512]{1,0:T(4,128)S(1)}, u32[]{:S(2)}, u32[]{:S(2)}) collective-permute-start(f32[3,512]{1,0:T(4,128)S(1)} %get-tuple-element.1062), channel_id=1, source_target_pairs={{0,1},{1,2},{2,3},{3,4},{4,5},{5,6},{6,7},{7,8},{8,9},{9,10},{10,1... | collective-permute-start | bytes 18440 | tf_op jit(solution)/shard_map/ppermute | solution.py:48
  139.9 5.5 %collective-permute-start.9 = (f32[3,512]{1,0:T(4,128)S(1)}, f32[3,512]{1,0:T(4,128)S(1)}, u32[]{:S(2)}, u32[]{:S(2)}) collective-permute-start(f32[3,512]{1,0:T(4,128)S(1)} %get-tuple-element.1063), channel_id=1, source_target_pairs={{1,0},{2,1},{3,2},{4,3},{5,4},{6,5},{7,6},{8,7},{9,8},{10,9},{11,1... | collective-permute-start | bytes 18440 | tf_op jit(solution)/shard_map/ppermute | solution.py:50
  144.0 28.8 %collective-permute-start.11 = (f32[2,2,3,128]{3,2,1,0:T(4,128)S(1)}, f32[2,2,3,128]{3,2,1,0:T(4,128)S(1)}, u32[]{:S(2)}, u32[]{:S(2)}) collective-permute-start(f32[2,2,3,128]{3,2,1,0:T(4,128)S(1)} %get-tuple-element.1080), channel_id=1, source_target_pairs={{0,2},{1,3},{2,0},{3,1},{4,6},{5,7},{6,4},{7,5},{8,10},{9,11},{10,... | collective-permute-start | bytes 18440 | tf_op jit(solution)/shard_map/ppermute | solution.py:30
  172.9 4.1 %collective-permute-start.12 = (f32[4,2,3,128]{3,2,1,0:T(4,128)S(1)}, f32[4,2,3,128]{3,2,1,0:T(4,128)S(1)}, u32[]{:S(2)}, u32[]{:S(2)}) collective-permute-start(f32[4,2,3,128]{3,2,1,0:T(4,128)S(1)} %bitcast.570), channel_id=1, source_target_pairs={{0,4},{1,5},{2,6},{3,7},{4,0},{5,1},{6,2},{7,3},{8,12},{9,13},{10,... | collective-permute-start | bytes 36872 | tf_op jit(solution)/shard_map/ppermute | solution.py:30
  177.0 4.8 %collective-permute-start.13 = (f32[8,2,3,128]{3,1,0,2:T(2,128)S(1)}, f32[8,2,3,128]{3,1,0,2:T(2,128)S(1)}, u32[]{:S(2)}, u32[]{:S(2)}) collective-permute-start(f32[8,2,3,128]{3,1,0,2:T(2,128)S(1)} %copy.44), channel_id=1, source_target_pairs={{0,8},{1,9},{2,10},{3,11},{4,12},{5,13},{6,14},{7,15},{8,0},{9,1},... | collective-permute-start | bytes 73736 | tf_op jit(solution)/shard_map/ppermute | solution.py:30
  294.2 5.0 %collective-permute-start.16 = (f32[1,2,3,128]{3,2,1,0:T(4,128)S(1)}, f32[1,2,3,128]{3,2,1,0:T(4,128)S(1)}, u32[]{:S(2)}, u32[]{:S(2)}) collective-permute-start(f32[1,2,3,128]{3,2,1,0:T(4,128)S(1)} %bitcast.762), channel_id=1, source_target_pairs={{0,1},{1,0},{2,3},{3,2},{4,5},{5,4},{6,7},{7,6},{8,9},{9,8},{10,11... | collective-permute-start | bytes 9224 | tf_op jit(solution)/shard_map/ppermute | solution.py:30
  294.6 5.8 %collective-permute-start.14 = (f32[3,512]{1,0:T(4,128)S(1)}, f32[3,512]{1,0:T(4,128)S(1)}, u32[]{:S(2)}, u32[]{:S(2)}) collective-permute-start(f32[3,512]{1,0:T(4,128)S(1)} %get-tuple-element.1054), channel_id=1, source_target_pairs={{0,1},{1,2},{2,3},{3,4},{4,5},{5,6},{6,7},{7,8},{8,9},{9,10},{10,1... | collective-permute-start | bytes 18440 | tf_op jit(solution)/shard_map/ppermute | solution.py:48
  295.1 5.5 %collective-permute-start.15 = (f32[3,512]{1,0:T(4,128)S(1)}, f32[3,512]{1,0:T(4,128)S(1)}, u32[]{:S(2)}, u32[]{:S(2)}) collective-permute-start(f32[3,512]{1,0:T(4,128)S(1)} %get-tuple-element.1055), channel_id=1, source_target_pairs={{1,0},{2,1},{3,2},{4,3},{5,4},{6,5},{7,6},{8,7},{9,8},{10,9},{11,1... | collective-permute-start | bytes 18440 | tf_op jit(solution)/shard_map/ppermute | solution.py:50
  299.3 28.8 %collective-permute-start.17 = (f32[2,2,3,128]{3,2,1,0:T(4,128)S(1)}, f32[2,2,3,128]{3,2,1,0:T(4,128)S(1)}, u32[]{:S(2)}, u32[]{:S(2)}) collective-permute-start(f32[2,2,3,128]{3,2,1,0:T(4,128)S(1)} %get-tuple-element.1078), channel_id=1, source_target_pairs={{0,2},{1,3},{2,0},{3,1},{4,6},{5,7},{6,4},{7,5},{8,10},{9,11},{10,... | collective-permute-start | bytes 18440 | tf_op jit(solution)/shard_map/ppermute | solution.py:30
  328.2 4.1 %collective-permute-start.18 = (f32[4,2,3,128]{3,2,1,0:T(4,128)S(1)}, f32[4,2,3,128]{3,2,1,0:T(4,128)S(1)}, u32[]{:S(2)}, u32[]{:S(2)}) collective-permute-start(f32[4,2,3,128]{3,2,1,0:T(4,128)S(1)} %bitcast.568), channel_id=1, source_target_pairs={{0,4},{1,5},{2,6},{3,7},{4,0},{5,1},{6,2},{7,3},{8,12},{9,13},{10,... | collective-permute-start | bytes 36872 | tf_op jit(solution)/shard_map/ppermute | solution.py:30
  332.3 4.8 %collective-permute-start.19 = (f32[8,2,3,128]{3,1,0,2:T(2,128)S(1)}, f32[8,2,3,128]{3,1,0,2:T(2,128)S(1)}, u32[]{:S(2)}, u32[]{:S(2)}) collective-permute-start(f32[8,2,3,128]{3,1,0,2:T(2,128)S(1)} %copy.49), channel_id=1, source_target_pairs={{0,8},{1,9},{2,10},{3,11},{4,12},{5,13},{6,14},{7,15},{8,0},{9,1},... | collective-permute-start | bytes 73736 | tf_op jit(solution)/shard_map/ppermute | solution.py:30
  (8 other events, 50.9 us)
